TPU v7x, 32 devices: a whole 2x2x4 slice. The times are simulated.
32 devices in a mesh: dp: 4 (over y, core), row: 2 (over x), col: 4 (over z).
Axes of the slice: x: 2, y: 2, z: 4, core: 2. Of those that a mesh axis runs over, the one named last changes fastest.
Arguments:
- block_in: bfloat16 [2048, 1024], P(('dp', 'row'), 'col'), may hold values from -6 to 6
- cotangent: bfloat16 [2048, 1024], P(('dp', 'row'), 'col'), may hold values from -6 to 6
- segments: int32 [2048], P('dp'), may hold values from 0 to 18, as said below
- positions: int32 [2048], P('dp'), may hold values from 0 to 511, as said below
- attn_gain: float32 [1024], P('col'), may hold values from 0.5 to 1.5
- attn_shift: float32 [1024], P('col'), may hold values from -1.5 to 1.5
- mlp_gain: float32 [1024], P('col'), may hold values from 0.5 to 1.5
- mlp_shift: float32 [1024], P('col'), may hold values from -1.5 to 1.5
- qkv_weight: bfloat16 [1024, 3072], P('col', 'row'), may hold values from -0.1875 to 0.1875
- qkv_bias: float32 [3072], P(('row', 'col')), may hold values from -2.5 to 2.5
- out_weight: bfloat16 [1024, 1024], P('row', 'col'), may hold values from -1.5 to 1.5
- out_bias: float32 [1024], P('col'), may hold values from -2.5 to 2.5
- up_weight: bfloat16 [1024, 4096], P('col', 'row'), may hold values from -0.1875 to 0.1875
- up_bias: float32 [4096], P(('row', 'col')), may hold values from -2.5 to 2.5
- down_weight: bfloat16 [4096, 1024], P('row', 'col'), may hold values from -0.09375 to 0.09375
- down_bias: float32 [1024], P('col'), may hold values from -2.5 to 2.5
Outputs:
- block_out: bfloat16 [2048, 1024], P(('dp', 'row'), 'col')
- grad_in: bfloat16 [2048, 1024], P(('dp', 'row'), 'col')
- grad_qkv_weight: float32 [1024, 3072], P('col', 'row')
- grad_qkv_bias: float32 [3072], P(('row', 'col'))
- grad_out_weight: float32 [1024, 1024], P('row', 'col')
- grad_out_bias: float32 [1024], P('col')
- grad_up_weight: float32 [1024, 4096], P('col', 'row')
- grad_up_bias: float32 [4096], P(('row', 'col'))
- grad_down_weight: float32 [4096, 1024], P('row', 'col')
- grad_down_bias: float32 [1024], P('col')
- grad_attn_gain: float32 [1024], P('col')
- grad_attn_shift: float32 [1024], P('col')
- grad_mlp_gain: float32 [1024], P('col')
- grad_mlp_shift: float32 [1024], P('col')
Inputs may be any that keep to these rules, and one draw needn't show every extreme that they name: segments never fall along the tokens, and every packed sequence of 512 tokens begins a new segment. `positions`: a token's position is the number of tokens before it in its segment.
All inputs are finite; a program needn't handle non-finite values.
Results may differ from a plain program's by a relative error of at most 0.011.
Values may be sent and summed in bfloat16 or wider, within the bound.
No kernel may reach another device: no remote copies, remote signals or barrier semaphores. Data moves between devices by JAX's collectives and lax.ppermute only.
A program may use at most 64 MiB of HBM per device.

v0:
```python
import math
import jax
import jax.numpy as jnp
from jax import lax
from jax.sharding import PartitionSpec as P

D = 1024
HD = 64
ROT = 16
EPS = 1e-05
NEG = -1e30


def rotary_tables(positions, rot_dims):
    half_dims = rot_dims // 2
    exponent = jnp.arange(half_dims, dtype=jnp.float32) * (2.0 / rot_dims)
    inverse = jnp.power(10000.0, -exponent)
    angles = positions.astype(jnp.float32)[:, None] * inverse[None, :]
    cosine = jnp.cos(angles)
    sine_tab = jnp.sin(angles)
    return (jnp.concatenate([cosine, cosine], 1), jnp.concatenate([sine_tab, sine_tab], 1))


def rotate_fwd(values, cosine, sine_tab):
    rot_dims = cosine.shape[1]
    half_dims = rot_dims // 2
    front = values[..., :rot_dims]
    turned = jnp.concatenate([-front[..., half_dims:], front[..., :half_dims]], -1)
    moved = front * cosine[:, None, :] + turned * sine_tab[:, None, :]
    return jnp.concatenate([moved, values[..., rot_dims:]], -1)


def rotate_back(grads, cosine, sine_tab):
    rot_dims = cosine.shape[1]
    half_dims = rot_dims // 2
    front = grads[..., :rot_dims]
    scaled = front * sine_tab[:, None, :]
    turned = jnp.concatenate([scaled[..., half_dims:], -scaled[..., :half_dims]], -1)
    moved = front * cosine[:, None, :] + turned
    return jnp.concatenate([moved, grads[..., rot_dims:]], -1)


def score_block(queries, keys_b, segments, start, width):
    length = keys_b.shape[0]
    raw = jnp.einsum("qhd,khd->hqk", queries, keys_b, preferred_element_type=jnp.float32) * (
        1.0 / math.sqrt(HD)
    )
    query_pos = start + jnp.arange(width, dtype=jnp.int32)
    key_pos = jnp.arange(length, dtype=jnp.int32)
    allowed = (key_pos[None, :] <= query_pos[:, None]) & (segments[None, :] == segments[:, None])
    return (jnp.where(allowed[None], raw, NEG), allowed)


def attend(queries, keys_b, values, segments):
    length, heads_here, head_dim = queries.shape
    width = min(512, length)
    count = length // width

    def one_block(index):
        start = index * width
        scores, allowed = score_block(queries, keys_b, segments, start, width)
        top = jnp.max(scores, -1, keepdims=True)
        expo = jnp.exp(scores - top)
        total = jnp.sum(expo, -1, keepdims=True)
        weights = (expo / total).astype(jnp.bfloat16)
        attended = jnp.einsum("hqk,khd->qhd", weights, values, preferred_element_type=jnp.float32)
        return (attended, (top + jnp.log(total))[..., 0])

    attended, log_total = lax.map(one_block, jnp.arange(count, dtype=jnp.int32))
    attended = attended.reshape(length, heads_here, head_dim)
    log_total = jnp.transpose(log_total, (1, 0, 2)).reshape(heads_here, length)
    return (attended, log_total)


def attend_back(queries, keys_b, values, grad_att, log_total, segments):
    length, heads_here, head_dim = queries.shape
    width = min(512, length)
    count = length // width
    scale = 1.0 / math.sqrt(HD)

    def one_block(carry, index):
        grad_keys, grad_values = carry
        start = index * width
        scores, allowed = score_block(queries, keys_b, segments, start, width)
        probs = jnp.where(allowed[None], jnp.exp(scores - log_total[..., None]), 0.0)
        probs_b = probs.astype(jnp.bfloat16)
        grad_values = grad_values + jnp.einsum(
            "hqk,qhd->khd", probs_b, grad_att, preferred_element_type=jnp.float32
        )
        grad_probs = jnp.einsum(
            "qhd,khd->hqk", grad_att, values, preferred_element_type=jnp.float32
        )
        delta = jnp.sum(probs * grad_probs, -1, keepdims=True)
        grad_scores = (probs * (grad_probs - delta) * scale).astype(jnp.bfloat16)
        grad_part = jnp.einsum(
            "hqk,khd->qhd", grad_scores, keys_b, preferred_element_type=jnp.float32
        )
        grad_keys = grad_keys + jnp.einsum(
            "hqk,qhd->khd", grad_scores, queries, preferred_element_type=jnp.float32
        )
        return ((grad_keys, grad_values), grad_part)

    zeros_kv = jnp.zeros((length, heads_here, head_dim), jnp.float32)
    (grad_keys, grad_values), grad_queries = lax.scan(
        one_block, (zeros_kv, zeros_kv), jnp.arange(count, dtype=jnp.int32)
    )
    return (grad_queries.reshape(length, heads_here, head_dim), grad_keys, grad_values)


def normal_cdf(values):
    return 0.5 * (1.0 + lax.erf(values * (1.0 / math.sqrt(2.0))))


def gelu_slope(values):
    return normal_cdf(values) + values * jnp.exp(-0.5 * values * values) * (
        1.0 / math.sqrt(2.0 * math.pi)
    )


def shards(
    block_in,
    cotangent,
    segments,
    positions,
    attn_gain,
    attn_shift,
    mlp_gain,
    mlp_shift,
    qkv_weight,
    qkv_bias,
    out_weight,
    out_bias,
    up_weight,
    up_bias,
    down_weight,
    down_bias,
):
    col_count = lax.axis_size("col")
    local_rows, local_width = block_in.shape
    length = segments.shape[0]
    qkv_share = qkv_weight.shape[1] // col_count
    up_share = up_weight.shape[1] // col_count
    heads_here = qkv_share // (3 * HD)
    att_width = heads_here * HD
    residual = block_in.astype(jnp.float32)
    totals = lax.psum((jnp.sum(residual, 1), jnp.sum(residual * residual, 1)), "col")
    average = totals[0][:, None] / D
    spread = totals[1][:, None] / D - average * average
    inv_std = lax.rsqrt(spread + EPS)
    normal = (residual - average) * inv_std
    normed = jnp.stack([normal * attn_gain + attn_shift, normal * mlp_gain + mlp_shift]).astype(
        jnp.bfloat16
    )
    normed_rows = lax.all_gather(normed, "row", axis=1, tiled=True)
    start = jnp.int32(0)
    blocks = []
    for offset in range(length * lax.axis_size("col") // length):
        piece_idx = start // length + offset
        qkv_part = lax.dynamic_slice_in_dim(qkv_weight, piece_idx * qkv_share, qkv_share, 1)
        up_part = lax.dynamic_slice_in_dim(up_weight, piece_idx * up_share, up_share, 1)
        blocks.append(
            jnp.concatenate(
                [
                    jnp.dot(normed_rows[0], qkv_part, preferred_element_type=jnp.float32),
                    jnp.dot(normed_rows[1], up_part, preferred_element_type=jnp.float32),
                ],
                1,
            )
        )
    first = lax.psum_scatter(jnp.concatenate(blocks, 0), "col", scatter_dimension=0, tiled=True)
    merged = first[:, :qkv_share] + qkv_bias
    up_proj = first[:, qkv_share:] + up_bias
    packed = merged.reshape(length, heads_here, 3, HD)
    cosine, sine_tab = rotary_tables(positions, ROT)
    queries = rotate_fwd(packed[:, :, 0], cosine, sine_tab).astype(jnp.bfloat16)
    keys_b = rotate_fwd(packed[:, :, 1], cosine, sine_tab).astype(jnp.bfloat16)
    values = packed[:, :, 2].astype(jnp.bfloat16)
    attended, log_total = attend(queries, keys_b, values, segments)
    attended = attended.reshape(length, att_width).astype(jnp.bfloat16)
    activated = (up_proj * normal_cdf(up_proj)).astype(jnp.bfloat16)
    mixed_cols = lax.all_gather(
        jnp.concatenate([attended, activated], 1), "col", axis=1, tiled=True
    )
    joined_grid = jnp.concatenate(
        [
            out_weight.reshape(col_count, att_width, local_width),
            down_weight.reshape(col_count, up_share, local_width),
        ],
        1,
    )
    joined = joined_grid.reshape(col_count * (att_width + up_share), local_width)
    mixed = lax.psum_scatter(
        jnp.dot(mixed_cols, joined, preferred_element_type=jnp.float32).astype(jnp.bfloat16),
        "row",
        scatter_dimension=0,
        tiled=True,
    ).astype(jnp.float32)
    block_out = (mixed + out_bias + down_bias + residual).astype(jnp.bfloat16)
    cot_rows = lax.all_gather(cotangent, "row", axis=0, tiled=True)
    grad_bias_out = jnp.sum(cot_rows.astype(jnp.float32), 0)
    grad_joined = jnp.dot(mixed_cols.T, cot_rows, preferred_element_type=jnp.float32)
    grad_joined = grad_joined.reshape(col_count, att_width + up_share, local_width)
    grad_out_w = grad_joined[:, :att_width].reshape(col_count * att_width, local_width)
    grad_down_w = grad_joined[:, att_width:].reshape(col_count * up_share, local_width)
    own_rows = lax.all_to_all(joined_grid, "col", split_axis=0, concat_axis=2, tiled=True)[0]
    cot_full = lax.all_gather(cot_rows, "col", axis=1, tiled=True)
    back = jnp.einsum("td,fd->tf", cot_full, own_rows, preferred_element_type=jnp.float32)
    grad_att = back[:, :att_width].astype(jnp.bfloat16).reshape(length, heads_here, HD)
    grad_up = back[:, att_width:] * gelu_slope(up_proj)
    grad_queries, grad_keys, grad_values = attend_back(
        queries, keys_b, values, grad_att, log_total, segments
    )
    grad_queries = rotate_back(grad_queries, cosine, sine_tab)
    grad_keys = rotate_back(grad_keys, cosine, sine_tab)
    grad_merged = jnp.stack([grad_queries, grad_keys, grad_values], 2).reshape(length, qkv_share)
    grad_qkv_b = jnp.sum(grad_merged, 0)
    grad_up_b = jnp.sum(grad_up, 0)
    first_back = jnp.concatenate(
        [grad_merged.astype(jnp.bfloat16), grad_up.astype(jnp.bfloat16)], 1
    )
    first_cols = lax.all_gather(first_back, "col", axis=1, tiled=True)
    split_cols = first_cols.reshape(length, col_count, qkv_share + up_share)
    merged_cols = split_cols[:, :, :qkv_share].reshape(length, col_count * qkv_share)
    up_cols = split_cols[:, :, qkv_share:].reshape(length, col_count * up_share)
    grad_qkv_w = jnp.dot(normed_rows[0].T, merged_cols, preferred_element_type=jnp.float32)
    grad_up_w = jnp.dot(normed_rows[1].T, up_cols, preferred_element_type=jnp.float32)
    up_part = up_cols
    grad_normed = lax.psum_scatter(
        jnp.stack(
            [
                jnp.dot(merged_cols, qkv_weight.T, preferred_element_type=jnp.float32),
                jnp.dot(up_part, up_weight.T, preferred_element_type=jnp.float32),
            ],
            1,
        ).astype(jnp.bfloat16),
        "row",
        scatter_dimension=0,
        tiled=True,
    ).astype(jnp.float32)
    grad_attn_in = grad_normed[:, 0]
    grad_mlp_in = grad_normed[:, 1]
    grad_normal = grad_attn_in * attn_gain + grad_mlp_in * mlp_gain
    grad_totals = lax.psum((jnp.sum(grad_normal, 1), jnp.sum(grad_normal * normal, 1)), "col")
    grad_x = cotangent.astype(jnp.float32) + inv_std * (
        grad_normal - grad_totals[0][:, None] / D - normal * (grad_totals[1][:, None] / D)
    )
    norm_params = lax.psum(
        (
            jnp.sum(grad_attn_in * normal, 0),
            jnp.sum(grad_attn_in, 0),
            jnp.sum(grad_mlp_in * normal, 0),
            jnp.sum(grad_mlp_in, 0),
        ),
        ("dp", "row"),
    )
    summed = (
        lax.psum(grad_qkv_w.astype(jnp.bfloat16), "dp").astype(jnp.float32),
        lax.psum(grad_qkv_b.astype(jnp.bfloat16), "dp").astype(jnp.float32),
        lax.psum(grad_out_w.astype(jnp.bfloat16), "dp").astype(jnp.float32),
        lax.psum(grad_bias_out.astype(jnp.bfloat16), "dp").astype(jnp.float32),
        lax.psum(grad_up_w.astype(jnp.bfloat16), "dp").astype(jnp.float32),
        lax.psum(grad_up_b.astype(jnp.bfloat16), "dp").astype(jnp.float32),
        lax.psum(grad_down_w.astype(jnp.bfloat16), "dp").astype(jnp.float32),
    )
    return (
        block_out,
        grad_x.astype(jnp.bfloat16),
        summed[0],
        summed[1],
        summed[2],
        summed[3],
        summed[4],
        summed[5],
        summed[6],
        summed[3],
        norm_params[0],
        norm_params[1],
        norm_params[2],
        norm_params[3],
    )


def solution(mesh):
    return jax.shard_map(
        shards,
        mesh=mesh,
        in_specs=(
            P(("dp", "row"), "col"),
            P(("dp", "row"), "col"),
            P("dp"),
            P("dp"),
            P("col"),
            P("col"),
            P("col"),
            P("col"),
            P("col", "row"),
            P(("row", "col")),
            P("row", "col"),
            P("col"),
            P("col", "row"),
            P(("row", "col")),
            P("row", "col"),
            P("col"),
        ),
        out_specs=(
            P(("dp", "row"), "col"),
            P(("dp", "row"), "col"),
            P("col", "row"),
            P(("row", "col")),
            P("row", "col"),
            P("col"),
            P("col", "row"),
            P(("row", "col")),
            P("row", "col"),
            P("col"),
            P("col"),
            P("col"),
            P("col"),
            P("col"),
        ),
        check_vma=False,
    )
```

profile of v0, /device:TPU:0, one launch (start us, length us, event | category | flops | bytes accessed | tf_op | source)
XLA Modules:
  0.0 464.6 jit_solution(14196637380774124360)
XLA Ops:
  7.2 9.1 %all_gather.17 = bf16[512,256]{1,0:T(8,128)(2,1)} all-gather(bf16[256,256]{1,0:T(8,128)(2,1)} %param.17), channel_id=1, replica_groups=mesh['dp'=4,'row'=2,'col'=4] {'row'}, dimensions={0}, use_global_device_ids=true | all-gather | bytes 393216 | tf_op jit(solution)/shard_map/all_gather | solution.py:199
  16.4 1.1 convert_reduce_fusion
  17.5 12.1 %all-reduce.2 = (f32[256]{0:T(256)S(1)}, f32[256]{0:T(256)S(1)}) all-reduce(f32[256]{0:T(256)S(1)} %get-tuple-element.74, f32[256]{0:T(256)S(1)} %get-tuple-element.73), channel_id=1, replica_groups=mesh['dp'=4,'row'=2,'col'=4] {'col'}, use_global_device_ids=true, to_apply=%region_3.0 | all-reduce | flops 512 | bytes 4096 | tf_op jit(solution)/shard_map/psum | solution.py:146
  29.6 1.1 fusion.69
  30.7 7.2 %all_gather.15 = bf16[2,512,256]{2,1,0:T(8,128)(2,1)S(1)} all-gather(bf16[2,256,256]{2,1,0:T(8,128)(2,1)S(1)} %pad_maximum_fusion.5), channel_id=1, replica_groups=mesh['dp'=4,'row'=2,'col'=4] {'row'}, dimensions={1}, use_global_device_ids=true | all-gather | bytes 786432 | tf_op jit(solution)/shard_map/all_gather | solution.py:154
  37.9 0.3 fusion.59
  38.9 0.3 fusion.51
  39.5 0.4 fusion.53
  39.9 0.4 fusion.55
  40.2 0.4 fusion.57
  40.6 8.6 %maximum_maximum_fusion = f32[2048,896]{0,1:T(8,128)} fusion(f32[512,512]{0,1:T(8,128)S(1)} %fusion.51, f32[512,384]{0,1:T(8,128)S(1)} %fusion.59, f32[512,512]{0,1:T(8,128)S(1)} %fusion.53, f32[512,384]{0,1:T(8,128)S(1)} %fusion.61, f32[512,512]{0,1:T(8,128)S(1)} %fusion.55, f32[512,384]{0,1:T(8,128)S(1)} %fusion.63, f32[512,512]{0,1:T(8,128)S(1)} %fusion.57, ...), kind=kLoop, calls=%fused_computation.1 | loop fusion | flops 12845056 | bytes 14680064 | tf_op jit(solution)/shard_map/concatenate | solution.py:170
  49.3 1.2 copy-done.9
  50.5 1.1 pad_maximum_fusion
  51.6 3.6 all-to-all-start
  55.7 0.9 fusion.27
  56.6 65.1 %all-to-all-done = bf16[4,640,256]{2,1,0:T(8,128)(2,1)S(1)} async-done(((bf16[4,640,256]{2,1,0:T(8,128)(2,1)}), bf16[4,640,256]{2,1,0:T(8,128)(2,1)S(1)}, u32[]{:S(2)}, u32[]{:S(2)}) %all-to-all-start) | async-done | bytes 1310752 | tf_op jit(solution)/shard_map/all_to_all | solution.py:205
  121.7 0.7 copy.59
  122.5 2.2 convolution_bitcast_fusion
  124.7 1.0 copy-done.6
  125.7 69.3 %reduce-scatter.4.cloned.1.call-done = f32[512,896]{0,1:T(8,128)} async-done(((f32[2048,896]{0,1:T(8,128)}), f32[512,896]{0,1:T(8,128)}) %reduce-scatter.4.cloned.1.call-update) | async-done | bytes 1835024 | tf_op jit(solution)/shard_map/reduce_scatter | solution.py:170
  195.0 1.2 slice_add_fusion.1
  196.5 0.6 fusion.94
  197.5 0.9 log_add_fusion
  198.5 0.5 fusion.74
  199.0 4.7 %fusion.12 = f32[512,2,64]{0,2,1:T(8,128)} fusion(f32[2,512,512]{1,2,0:T(8,128)S(1)} %fusion.74, f32[2,512,512]{1,2,0:T(8,128)} %copy-done.4, f32[2,512]{1,0:T(2,128)} %log_add_fusion, pred[512,512]{0,1:T(8,128)(4,1)} %fusion.27, bf16[512,2,48]{0,2,1:T(8,128)(2,1)} %copy-done.26, bf16[512,2,16]{0,2,1:T(8,128)(2,1)} %copy-done.29), kind=kOutput, calls=%fused_computation.22 | convolution fusion | flops 72091136 | bytes 4853760 | tf_op jit(solution)/shard_map/while/body/eval_jaxpr/hqk,khd->qhd/dot_general | solution.py:95
  203.6 4.7 %fusion.15 = f32[512,2,64]{0,2,1:T(8,128)} fusion(f32[2,512,512]{1,2,0:T(8,128)S(1)} %fusion.74, f32[2,512,512]{1,2,0:T(8,128)} %copy-done.4, f32[2,512]{1,0:T(2,128)} %log_add_fusion, pred[512,512]{0,1:T(8,128)(4,1)} %fusion.27, bf16[512,2,48]{0,2,1:T(8,128)(2,1)} %copy-done.27, bf16[512,2,16]{0,2,1:T(8,128)(2,1)} %copy-done.28), kind=kOutput, calls=%fused_computation.23 | convolution fusion | flops 72091136 | bytes 4853760 | tf_op jit(solution)/shard_map/while/body/eval_jaxpr/hqk,qhd->khd/dot_general | solution.py:98
  208.3 1.0 slice_multiply_fusion.3
  209.3 2.2 convolution_bitcast_fusion.1
  211.8 0.5 copy-done.10
  212.3 0.8 copy-done.5
  213.1 0.4 copy-done.7
  213.5 0.7 fusion.88
  214.2 1.0 pad_maximum_fusion.1
  215.3 2.1 convolution_convert_fusion.6
  217.3 0.9 pad_maximum_fusion.3
  218.3 74.6 %all-gather.8.cloned.1.call-done = bf16[512,3584]{0,1:T(8,128)(2,1)} async-done(((bf16[512,896]{0,1:T(8,128)(2,1)}), bf16[512,3584]{0,1:T(8,128)(2,1)}) %all-gather.8.cloned.1.call-update) | async-done | bytes 3670032 | tf_op jit(solution)/shard_map/all_gather | solution.py:221
  292.9 1.7 slice.176
  294.6 1.6 slice.175
  296.2 0.6 fusion.11
  296.9 1.1 copy-done.13
  298.0 0.8 fusion.18
  298.8 0.8 pad_maximum_fusion.4
  299.7 48.5 %all-gather.4.cloned.1.call-done = bf16[512,2560]{0,1:T(8,128)(2,1)} async-done(((bf16[512,640]{0,1:T(8,128)(2,1)}), bf16[512,2560]{0,1:T(8,128)(2,1)}) %all-gather.4.cloned.1.call-update) | async-done | bytes 2621456 | tf_op jit(solution)/shard_map/all_gather | solution.py:181
  348.2 2.6 convolution_convert_fusion
  350.8 1.0 slice.180
  351.8 0.7 slice.179
  352.6 0.4 copy-done.1
  353.0 2.9 convolution_convert_fusion.3
  356.2 2.9 convolution_convert_fusion.2
  359.1 1.7 convolution_convert_fusion.1
  361.0 0.8 copy-done.11
  362.0 6.4 %all-reduce.3 = (bf16[384]{0:T(512)(128)(2,1)S(1)}, bf16[256]{0:T(256)(128)(2,1)S(1)}, bf16[512]{0:T(512)(128)(2,1)S(1)}) all-reduce(bf16[384]{0:T(512)(128)(2,1)S(1)} %convert_element_type.134, bf16[256]{0:T(256)(128)(2,1)S(1)} %reduce_sum.129, bf16[512]{0:T(512)(128)(2,1)S(1)} %get-tuple-element.90), channel_id=1, replica_groups=mesh['dp'=4,'row'=2,'col'=4] {'dp'}, use_global_device_ids=true, to_apply=%region_16.17 | all-reduce | flops 1152 | bytes 4608 | tf_op jit(solution)/shard_map/psum | solution.py:258
  368.4 0.6 convert_element_type.135
  369.0 0.6 convert_element_type.142
  369.6 1.0 convert_element_type.129
  370.9 14.2 %all-reduce = (f32[256]{0:T(256)}, f32[256]{0:T(256)}, f32[256]{0:T(256)}, f32[256]{0:T(256)}) all-reduce(f32[256]{0:T(256)S(1)} %get-tuple-element.71, f32[256]{0:T(256)S(1)} %get-tuple-element.68, f32[256]{0:T(256)S(1)} %get-tuple-element.72, f32[256]{0:T(256)S(1)} %get-tuple-element.57), channel_id=1, replica_groups=mesh['dp'=4,'row'=2,'col'=4] {'dp','row'}, use_global_device_ids=true, to_apply=%region_25.26 | all-reduce | flops 1024 | bytes 8192 | tf_op jit(solution)/shard_map/psum | solution.py:247
  385.1 9.7 %all-reduce.1 = (f32[256]{0:T(256)S(1)}, f32[256]{0:T(256)S(1)}) all-reduce(f32[256]{0:T(256)S(1)} %get-tuple-element.70, f32[256]{0:T(256)S(1)} %get-tuple-element.69), channel_id=1, replica_groups=mesh['dp'=4,'row'=2,'col'=4] {'col'}, use_global_device_ids=true, to_apply=%region_13.14 | all-reduce | flops 512 | bytes 4096 | tf_op jit(solution)/shard_map/psum | solution.py:243
  394.9 1.8 fusion.45
  396.7 54.0 %all-reduce.7.cloned.1.call-done = (bf16[256,1536]{1,0:T(8,128)(2,1)}, bf16[512,256]{1,0:T(8,128)(2,1)}, bf16[256,2048]{1,0:T(8,128)(2,1)}, bf16[2048,256]{1,0:T(8,128)(2,1)}) async-done(((bf16[256,1536]{1,0:T(8,128)(2,1)}, bf16[512,256]{1,0:T(8,128)(2,1)}, bf16[256,2048]{1,0:T(8,128)(2,1)}, bf16[2048,256]{1,0:T(8,128)(2,1)}), (bf16[256,1536]{1,0:T(8,128)(2,1)}, bf16[512,256]{1,0:T(8,128)(2,1)}, ...) | async-done | bytes 3145744 | tf_op jit(solution)/shard_map/psum | solution.py:257
  450.6 2.9 convert_element_type.140
  453.5 1.5 convert_element_type.144
  455.0 1.3 convert_element_type.132
  456.3 0.8 convert_element_type.137
  457.2 0.6 copy.84
  (125 shorter events, 3.6 us)
Async XLA Ops:
  7.2 30.7 %copy-start.14 = (bf16[256,1536]{1,0:T(8,128)(2,1)S(1)}, bf16[256,1536]{1,0:T(8,128)(2,1)}, u32[]{:S(2)}) copy-start(bf16[256,1536]{1,0:T(8,128)(2,1)} %param.24) | copy-start | bytes 2359300
  7.2 115.3 %all-gather.6.cloned.1.call-start = ((), (), s32[]{:S(2)}) async-start(), calls=%async_computation.7 | async-start | bytes 1310720 | tf_op jit(solution)/shard_map/all_gather | solution.py:206
  16.4 178.6 %reduce-scatter.4.cloned.1.call-start = ((), (), s32[]{:S(2)}) async-start(), calls=%async_computation.4 | async-start | bytes 9175040 | tf_op jit(solution)/shard_map/reduce_scatter | solution.py:170
  30.7 8.1 %copy-start.12 = (bf16[256,2048]{1,0:T(8,128)(2,1)S(1)}, bf16[256,2048]{1,0:T(8,128)(2,1)}, u32[]{:S(2)}) copy-start(bf16[256,2048]{1,0:T(8,128)(2,1)} %param.28) | copy-start | bytes 3145732
  49.2 1.2 copy-start.9
  49.2 1.3 copy-start.23
  50.5 5.0 %copy-start.35 = (s32[512]{0:T(512)S(1)}, s32[512]{0:T(512)}, u32[]{:S(2)}) copy-start(s32[512]{0:T(512)} %param.19) | copy-start | bytes 6148
  50.5 5.2 %copy-start.30 = (s32[512]{0:T(512)S(1)}, s32[512]{0:T(512)}, u32[]{:S(2)}) copy-start(s32[512]{0:T(512)} %param.18) | copy-start | bytes 6148
  51.6 70.1 %all-to-all-start = ((bf16[4,640,256]{2,1,0:T(8,128)(2,1)}), bf16[4,640,256]{2,1,0:T(8,128)(2,1)S(1)}, u32[]{:S(2)}, u32[]{:S(2)}) async-start(bf16[4,640,256]{2,1,0:T(8,128)(2,1)} %pad_maximum_fusion), calls=%async_computation.2 | async-start | bytes 2621440 | tf_op jit(solution)/shard_map/all_to_all | solution.py:205
  55.3 237.6 %all-gather.8.cloned.1.call-start = ((), (), s32[]{:S(2)}) async-start(), calls=%async_computation.8 | async-start | bytes 4587520 | tf_op jit(solution)/shard_map/all_gather | solution.py:221
  55.7 140.7 %copy-start.20 = (f32[512,16]{0,1:T(8,128)}, f32[512,16]{0,1:T(8,128)S(1)}, u32[]{:S(2)}) copy-start(f32[512,16]{0,1:T(8,128)S(1)} %get-tuple-element.123) | copy-start | bytes 98308
  55.7 140.7 %copy-start.21 = (f32[512,16]{0,1:T(8,128)}, f32[512,16]{0,1:T(8,128)S(1)}, u32[]{:S(2)}) copy-start(f32[512,16]{0,1:T(8,128)S(1)} %get-tuple-element.122) | copy-start | bytes 98308
  122.5 72.5 %copy-start.33 = (f32[384]{0:T(512)S(1)}, f32[384]{0:T(512)}, u32[]{:S(2)}) copy-start(f32[384]{0:T(512)} %param.25) | copy-start | bytes 4612
  124.7 1.1 copy-start.6
  125.7 70.8 %copy-start.25 = (pred[512,512]{0,1:T(8,128)(4,1)S(1)}, pred[512,512]{0,1:T(8,128)(4,1)}, u32[]{:S(2)}) copy-start(pred[512,512]{0,1:T(8,128)(4,1)} %fusion.27) | copy-start | bytes 786436
  196.4 1.1 copy-start.26
  196.4 1.1 copy-start.27
  196.5 1.0 copy-start.28
  196.5 1.0 copy-start.29
  197.2 1.3 copy-start.4
  208.3 3.3 copy-start.16
  208.3 3.3 copy-start.17
  208.3 3.3 copy-start.22
  208.3 3.3 slice-start
  209.3 2.4 slice-start.1
  211.5 0.7 copy-start.10
  211.5 1.6 copy-start.5
  211.5 2.0 copy-start.7
  211.6 1.9 copy-start.34
  215.2 133.0 %all-gather.4.cloned.1.call-start = ((), (), s32[]{:S(2)}) async-start(), calls=%async_computation.5 | async-start | bytes 3276800 | tf_op jit(solution)/shard_map/all_gather | solution.py:181
  218.2 151.4 %reduce-scatter.8.cloned.1.call-start = ((), (), s32[]{:S(2)}) async-start(), calls=%async_computation.9 | async-start | bytes 786432 | tf_op jit(solution)/shard_map/reduce_scatter | solution.py:228
  294.6 1.6 copy-start.15
  296.2 2.6 copy-start
  296.2 1.8 copy-start.13
  298.0 50.2 %copy-start.2 = (bf16[512,256]{1,0:T(8,128)(2,1)S(1)}, bf16[512,256]{1,0:T(8,128)(2,1)}, u32[]{:S(2)}) copy-start(bf16[512,256]{1,0:T(8,128)(2,1)} %all_gather.17) | copy-start | bytes 786436
  299.7 95.2 %reduce-scatter.6.cloned.1.call-start = ((), (), s32[]{:S(2)}) async-start(), calls=%async_computation.6 | async-start | bytes 393216 | tf_op jit(solution)/shard_map/reduce_scatter | solution.py:192
  350.8 2.2 copy-start.1
  355.9 94.7 %all-reduce.7.cloned.1.call-start = ((), (), s32[]{:S(2)}) async-start(), calls=%async_computation.10 | async-start | bytes 6291456 | tf_op jit(solution)/shard_map/psum | solution.py:257
  360.9 0.9 copy-start.11
  360.9 9.8 %copy-start.3 = (bf16[256,256]{1,0:T(8,128)(2,1)S(1)}, bf16[256,256]{1,0:T(8,128)(2,1)}, u32[]{:S(2)}) copy-start(bf16[256,256]{1,0:T(8,128)(2,1)} %param.16) | copy-start | bytes 393220
  360.9 9.8 %copy-start.31 = (f32[256]{0:T(256)S(1)}, f32[256]{0:T(256)}, u32[]{:S(2)}) copy-start(f32[256]{0:T(256)} %param.20) | copy-start | bytes 3076
  360.9 9.8 %copy-start.32 = (f32[256]{0:T(256)S(1)}, f32[256]{0:T(256)}, u32[]{:S(2)}) copy-start(f32[256]{0:T(256)} %param.22) | copy-start | bytes 3076
  360.9 34.0 %copy-start.19 = (bf16[256,256]{1,0:T(8,128)(2,1)S(1)}, bf16[256,256]{1,0:T(8,128)(2,1)}, u32[]{:S(2)}) copy-start(bf16[256,256]{1,0:T(8,128)(2,1)} %param.17) | copy-start | bytes 393220
  360.9 34.0 %copy-start.36 = (f32[256]{0:T(256)S(1)}, f32[256]{0:T(256)}, u32[]{:S(2)}) copy-start(f32[256]{0:T(256)} %param.31) | copy-start | bytes 3076
  360.9 34.0 %copy-start.37 = (f32[256]{0:T(256)S(1)}, f32[256]{0:T(256)}, u32[]{:S(2)}) copy-start(f32[256]{0:T(256)} %param.27) | copy-start | bytes 3076
  369.6 87.6 %copy-start.38 = (f32[256]{0:T(256)}, f32[256]{0:T(256)S(1)}, u32[]{:S(2)}) copy-start(f32[256]{0:T(256)S(1)} %convert_element_type.138) | copy-start | bytes 3076
  450.6 2.9 copy-start.8
  453.5 1.5 copy-start.18
  453.5 2.8 copy-start.24
Sparse Core Ops, SparseCore 0:
  16.5 30.1 all-gather.5
  49.4 145.5 reduce-scatter.3
  215.3 77.4 all-gather.7
  294.9 53.2 all-gather.3
  350.9 13.3 reduce-scatter.7
  366.4 11.9 reduce-scatter.5
  382.1 68.5 all-reduce.6
where the time goes:
time: 465 us
  waiting for transfers between devices  312 us (67%)
  blocking collectives  58.6 us (13%)
  other arithmetic  31 us (7%)
  matrix products  31 us (7%)
  between operations  14.8 us (3%)
  local copies, waits for them, and re-layouts  13.2 us (3%)
    all_gather x1, waiting for transfers between devices, shards(): first_cols = lax.all_gather(first_back, 'col', axis=1, tiled=True)  74.6 us
    reduce_scatter x1, waiting for transfers between devices, shards(): lax.psum_scatter(jnp.concatenate(blocks, 0), 'col', scatter_dimension=0,...  69.3 us
    all_to_all x1, waiting for transfers between devices, shards(): lax.all_to_all(joined_grid, 'col', split_axis=0, concat_axis=2, tiled=True)  65.1 us
    psum x1, waiting for transfers between devices, shards(): lax.psum(grad_qkv_w.astype(jnp.bfloat16), 'dp').astype(jnp.float32)  54 us
    all_gather x1, waiting for transfers between devices, shards(): lax.all_gather(jnp.concatenate([attended, activated], 1), 'col', axis=1,...  48.5 us
    psum x1, blocking collectives, shards(): lax.psum((jnp.sum(grad_attn_in * normal, 0), jnp.sum(grad_attn_in, 0), jn...  14.2 us
    psum x1, blocking collectives, shards(): lax.psum((jnp.sum(residual, 1), jnp.sum(residual * residual, 1)), 'col')  12.1 us
    psum x1, blocking collectives, shards(): lax.psum((jnp.sum(grad_normal, 1), jnp.sum(grad_normal * normal, 1)), 'col')  9.68 us
  transfers between devices with their start and end apart: 8, of which 5 were waited for; matrix products, arithmetic and copies ran while one was open for 9% of the time, Pallas kernels for 0%

commit v1 on v0

--- a/solution.py
+++ b/solution.py
@@ -135,6 +135,18 @@
     down_weight,
     down_bias,
 ):
+
+    def supply_all_area_in(field_in, dev_axis, dim_no):
+        lanes = []
+        for _ in range(lax.axis_size(dev_axis)):
+            lanes.append(field_in)
+        return jnp.concatenate(
+            lax.all_to_all(
+                jnp.stack(lanes, axis=0), axis_name=dev_axis, split_axis=0, concat_axis=0
+            ),
+            dim_no,
+        )
+
     col_count = lax.axis_size("col")
     local_rows, local_width = block_in.shape
     length = segments.shape[0]
@@ -178,9 +190,7 @@
     attended, log_total = attend(queries, keys_b, values, segments)
     attended = attended.reshape(length, att_width).astype(jnp.bfloat16)
     activated = (up_proj * normal_cdf(up_proj)).astype(jnp.bfloat16)
-    mixed_cols = lax.all_gather(
-        jnp.concatenate([attended, activated], 1), "col", axis=1, tiled=True
-    )
+    mixed_cols = supply_all_area_in(jnp.concatenate([attended, activated], 1), "col", 1)
     joined_grid = jnp.concatenate(
         [
             out_weight.reshape(col_count, att_width, local_width),

time: 465 us -> 470 us (1.011)
  starting transfers between devices: 4.32 us -> 14 us
  waiting for transfers between devices: 312 us -> 303 us
  local copies, waits for them, and re-layouts: 13.2 us -> 18.3 us
    all_gather x1 -> x0, waiting for transfers between devices: 48.5 us -> none  [shards(): lax.all_gather(jnp.concatenate([attended, activated], 1), 'col', axis=1,...]
    all_gather x1, waiting for transfers between devices: 74.6 us -> 119 us  [shards(): first_cols = lax.all_gather(first_back, 'col', axis=1, tiled=True)]
    all_to_all x0 -> x1, starting transfers between devices: none -> 9.76 us  [supply_all_area_in(): lax.all_to_all(jnp.stack(lanes, axis=0), axis_name=dev_axis, split_axis=0...]
  transfers between devices with their start and end apart: 8 -> 8, of which waited for: 5 -> 4; matrix products, arithmetic and copies ran while one was open for 9% -> 10% of each run, Pallas kernels for 0% -> 0%
where the time goes in v1:
time: 470 us; the launch traced here: 469 us
  waiting for transfers between devices  303 us (64%)
  blocking collectives  59 us (13%)
  other arithmetic  30.3 us (6%)
  matrix products  29.9 us (6%)
  local copies, waits for them, and re-layouts  18.3 us (4%)
  between operations  14.9 us (3%)
  starting transfers between devices  14 us (3%)
    all_gather x1, waiting for transfers between devices, shards(): first_cols = lax.all_gather(first_back, 'col', axis=1, tiled=True)  119 us
    reduce_scatter x1, waiting for transfers between devices, shards(): lax.psum_scatter(jnp.concatenate(blocks, 0), 'col', scatter_dimension=0,...  69.2 us
    all_to_all x1, waiting for transfers between devices, shards(): lax.all_to_all(joined_grid, 'col', split_axis=0, concat_axis=2, tiled=True)  65.1 us
    psum x1, waiting for transfers between devices, shards(): lax.psum(grad_qkv_w.astype(jnp.bfloat16), 'dp').astype(jnp.float32)  49.3 us
    psum x1, blocking collectives, shards(): lax.psum((jnp.sum(grad_attn_in * normal, 0), jnp.sum(grad_attn_in, 0), jn...  13.2 us
    psum x1, blocking collectives, shards(): lax.psum((jnp.sum(residual, 1), jnp.sum(residual * residual, 1)), 'col')  12.1 us
    psum x1, blocking collectives, shards(): lax.psum((jnp.sum(grad_normal, 1), jnp.sum(grad_normal * normal, 1)), 'col')  10.6 us
    all_to_all x1, starting transfers between devices, supply_all_area_in(): lax.all_to_all(jnp.stack(lanes, axis=0), axis_name=dev_axis, split_axis=0...  9.76 us
  transfers between devices with their start and end apart: 8, of which 4 were waited for; matrix products, arithmetic and copies ran while one was open for 10% of the time, Pallas kernels for 0%

profile of v1, /device:TPU:0, one launch (start us, length us, event | category | flops | bytes accessed | tf_op | source)
XLA Modules:
  0.0 469.3 jit_solution(7831227692561734413)
XLA Ops:
  7.2 9.1 %all_gather.13 = bf16[512,256]{1,0:T(8,128)(2,1)} all-gather(bf16[256,256]{1,0:T(8,128)(2,1)} %param.17), channel_id=1, replica_groups=mesh['dp'=4,'row'=2,'col'=4] {'row'}, dimensions={0}, use_global_device_ids=true | all-gather | bytes 393216 | tf_op jit(solution)/shard_map/all_gather | solution.py:209
  16.4 1.1 convert_reduce_fusion
  17.5 12.1 %all-reduce.2 = (f32[256]{0:T(256)S(1)}, f32[256]{0:T(256)S(1)}) all-reduce(f32[256]{0:T(256)S(1)} %get-tuple-element.74, f32[256]{0:T(256)S(1)} %get-tuple-element.73), channel_id=1, replica_groups=mesh['dp'=4,'row'=2,'col'=4] {'col'}, use_global_device_ids=true, to_apply=%region_3.0 | all-reduce | flops 512 | bytes 4096 | tf_op jit(solution)/shard_map/psum | solution.py:158
  29.6 1.1 fusion.76
  30.7 7.2 %all_gather.12 = bf16[2,512,256]{2,1,0:T(8,128)(2,1)S(1)} all-gather(bf16[2,256,256]{2,1,0:T(8,128)(2,1)S(1)} %pad_maximum_fusion.5), channel_id=1, replica_groups=mesh['dp'=4,'row'=2,'col'=4] {'row'}, dimensions={1}, use_global_device_ids=true | all-gather | bytes 786432 | tf_op jit(solution)/shard_map/all_gather | solution.py:166
  38.5 0.3 fusion.70
  38.9 0.4 fusion.58
  39.5 0.4 fusion.60
  39.9 0.4 fusion.62
  40.2 0.4 fusion.64
  40.6 8.7 %maximum_maximum_fusion = f32[2048,896]{0,1:T(8,128)} fusion(f32[512,512]{0,1:T(8,128)S(1)} %fusion.58, f32[512,384]{0,1:T(8,128)S(1)} %fusion.66, f32[512,512]{0,1:T(8,128)S(1)} %fusion.60, f32[512,384]{0,1:T(8,128)S(1)} %fusion.68, f32[512,512]{0,1:T(8,128)S(1)} %fusion.62, f32[512,384]{0,1:T(8,128)S(1)} %fusion.70, f32[512,512]{0,1:T(8,128)S(1)} %fusion.64, ...), kind=kLoop, calls=%fused_computation.1 | loop fusion | flops 12845056 | bytes 14680064 | tf_op jit(solution)/shard_map/concatenate | solution.py:182
  49.3 1.2 copy-done.14
  50.5 1.1 pad_maximum_fusion
  51.7 3.6 all-to-all-start.1
  55.8 0.9 fusion.33
  56.7 65.1 %all-to-all-done.1 = bf16[4,640,256]{2,1,0:T(8,128)(2,1)S(1)} async-done(((bf16[4,640,256]{2,1,0:T(8,128)(2,1)}), bf16[4,640,256]{2,1,0:T(8,128)(2,1)S(1)}, u32[]{:S(2)}, u32[]{:S(2)}) %all-to-all-start.1) | async-done | bytes 1310752 | tf_op jit(solution)/shard_map/all_to_all | solution.py:215
  121.8 0.7 copy.55
  122.5 2.2 convolution_bitcast_fusion
  124.7 1.0 copy-done.11
  125.8 69.2 %reduce-scatter.4.cloned.1.call-done = f32[512,896]{0,1:T(8,128)} async-done(((f32[2048,896]{0,1:T(8,128)}), f32[512,896]{0,1:T(8,128)}) %reduce-scatter.4.cloned.1.call-update) | async-done | bytes 1835024 | tf_op jit(solution)/shard_map/reduce_scatter | solution.py:182
  195.0 1.2 slice_add_fusion.1
  196.6 0.6 fusion.102
  197.6 1.0 log_add_fusion
  198.6 0.5 fusion.81
  199.1 4.7 fusion.18
  203.7 4.7 fusion.21
  208.4 1.0 slice_multiply_fusion.3
  209.4 2.2 convolution_bitcast_fusion.2
  211.8 0.5 copy-done.16
  212.6 0.6 copy-done.6
  213.3 0.5 copy-done.12
  213.8 0.7 fusion.96
  214.5 1.0 pad_maximum_fusion.1
  215.5 2.1 convolution_convert_fusion.4
  217.9 1.7 stack.46
  219.6 9.8 %all-to-all-start = ((bf16[4,512,640]{2,1,0:T(8,128)(2,1)}), bf16[4,512,640]{2,1,0:T(8,128)(2,1)S(1)}, u32[]{:S(2)}, u32[]{:S(2)}) async-start(bf16[4,512,640]{2,1,0:T(8,128)(2,1)} %stack.46), calls=%async_computation.1 | async-start | bytes 5242880 | tf_op jit(solution)/shard_map/all_to_all | solution.py:144
  229.4 119.0 %all-gather.5.cloned.1.call-done = bf16[512,3584]{0,1:T(8,128)(2,1)} async-done(((bf16[512,896]{0,1:T(8,128)(2,1)}), bf16[512,3584]{0,1:T(8,128)(2,1)}) %all-gather.5.cloned.1.call-update) | async-done | bytes 3670032 | tf_op jit(solution)/shard_map/all_gather | solution.py:231
  348.4 1.7 slice.176
  350.2 2.3 slice.175
  352.5 0.6 fusion.17
  353.2 1.1 copy-done.19
  354.3 0.8 fusion.24
  355.1 0.8 pad_maximum_fusion.4
  356.2 2.7 copy.61
  358.9 2.6 fusion.13
  361.5 1.0 slice.180
  362.5 0.7 slice.179
  363.2 1.6 fusion.16
  364.9 3.1 convolution_convert_fusion.1
  368.0 1.7 convolution_convert_fusion
  369.9 0.8 copy-done.5
  371.0 6.9 %all-reduce.3 = (bf16[384]{0:T(512)(128)(2,1)S(1)}, bf16[256]{0:T(256)(128)(2,1)S(1)}, bf16[512]{0:T(512)(128)(2,1)S(1)}) all-reduce(bf16[384]{0:T(512)(128)(2,1)S(1)} %convert_element_type.134, bf16[256]{0:T(256)(128)(2,1)S(1)} %reduce_sum.129, bf16[512]{0:T(512)(128)(2,1)S(1)} %get-tuple-element.90), channel_id=1, replica_groups=mesh['dp'=4,'row'=2,'col'=4] {'dp'}, use_global_device_ids=true, to_apply=%region_16.17 | all-reduce | flops 1152 | bytes 4608 | tf_op jit(solution)/shard_map/psum | solution.py:268
  377.9 0.6 convert_element_type.135
  378.5 0.6 convert_element_type.142
  379.1 1.0 convert_element_type.129
  380.4 13.2 %all-reduce = (f32[256]{0:T(256)}, f32[256]{0:T(256)}, f32[256]{0:T(256)}, f32[256]{0:T(256)}) all-reduce(f32[256]{0:T(256)S(1)} %get-tuple-element.71, f32[256]{0:T(256)S(1)} %get-tuple-element.68, f32[256]{0:T(256)S(1)} %get-tuple-element.72, f32[256]{0:T(256)S(1)} %get-tuple-element.57), channel_id=1, replica_groups=mesh['dp'=4,'row'=2,'col'=4] {'dp','row'}, use_global_device_ids=true, to_apply=%region_25.26 | all-reduce | flops 1024 | bytes 8192 | tf_op jit(solution)/shard_map/psum | solution.py:257
  393.6 10.6 %all-reduce.1 = (f32[256]{0:T(256)S(1)}, f32[256]{0:T(256)S(1)}) all-reduce(f32[256]{0:T(256)S(1)} %get-tuple-element.70, f32[256]{0:T(256)S(1)} %get-tuple-element.69), channel_id=1, replica_groups=mesh['dp'=4,'row'=2,'col'=4] {'col'}, use_global_device_ids=true, to_apply=%region_13.14 | all-reduce | flops 512 | bytes 4096 | tf_op jit(solution)/shard_map/psum | solution.py:253
  404.2 1.8 fusion.51
  406.0 49.3 %all-reduce.7.cloned.1.call-done = (bf16[256,1536]{1,0:T(8,128)(2,1)}, bf16[512,256]{1,0:T(8,128)(2,1)}, bf16[256,2048]{1,0:T(8,128)(2,1)}, bf16[2048,256]{1,0:T(8,128)(2,1)}) async-done(((bf16[256,1536]{1,0:T(8,128)(2,1)}, bf16[512,256]{1,0:T(8,128)(2,1)}, bf16[256,2048]{1,0:T(8,128)(2,1)}, bf16[2048,256]{1,0:T(8,128)(2,1)}), (bf16[256,1536]{1,0:T(8,128)(2,1)}, bf16[512,256]{1,0:T(8,128)(2,1)}, ...) | async-done | bytes 3145744 | tf_op jit(solution)/shard_map/psum | solution.py:267
  455.4 2.9 convert_element_type.140
  458.2 1.5 convert_element_type.144
  459.7 1.3 convert_element_type.132
  461.1 0.8 convert_element_type.137
  461.9 0.6 copy.81
  (141 shorter events, 4.2 us)
Async XLA Ops:
  7.2 30.7 %copy-start.20 = (bf16[256,1536]{1,0:T(8,128)(2,1)S(1)}, bf16[256,1536]{1,0:T(8,128)(2,1)}, u32[]{:S(2)}) copy-start(bf16[256,1536]{1,0:T(8,128)(2,1)} %param.24) | copy-start | bytes 2359300
  7.2 115.3 %all-gather.3.cloned.1.call-start = ((), (), s32[]{:S(2)}) async-start(), calls=%async_computation.7 | async-start | bytes 1310720 | tf_op jit(solution)/shard_map/all_gather | solution.py:216
  16.4 178.6 %reduce-scatter.4.cloned.1.call-start = ((), (), s32[]{:S(2)}) async-start(), calls=%async_computation.5 | async-start | bytes 9175040 | tf_op jit(solution)/shard_map/reduce_scatter | solution.py:182
  30.7 8.1 %copy-start.18 = (bf16[256,2048]{1,0:T(8,128)(2,1)S(1)}, bf16[256,2048]{1,0:T(8,128)(2,1)}, u32[]{:S(2)}) copy-start(bf16[256,2048]{1,0:T(8,128)(2,1)} %param.28) | copy-start | bytes 3145732
  49.3 1.2 copy-start.14
  49.3 1.3 copy-start.29
  50.5 5.0 %copy-start.42 = (s32[512]{0:T(512)S(1)}, s32[512]{0:T(512)}, u32[]{:S(2)}) copy-start(s32[512]{0:T(512)} %param.19) | copy-start | bytes 6148
  50.5 5.2 %copy-start.37 = (s32[512]{0:T(512)S(1)}, s32[512]{0:T(512)}, u32[]{:S(2)}) copy-start(s32[512]{0:T(512)} %param.18) | copy-start | bytes 6148
  51.7 70.1 %all-to-all-start.1 = ((bf16[4,640,256]{2,1,0:T(8,128)(2,1)}), bf16[4,640,256]{2,1,0:T(8,128)(2,1)S(1)}, u32[]{:S(2)}, u32[]{:S(2)}) async-start(bf16[4,640,256]{2,1,0:T(8,128)(2,1)} %pad_maximum_fusion), calls=%async_computation.3 | async-start | bytes 2621440 | tf_op jit(solution)/shard_map/all_to_all | solution.py:215
  55.3 293.1 %all-gather.5.cloned.1.call-start = ((), (), s32[]{:S(2)}) async-start(), calls=%async_computation.8 | async-start | bytes 4587520 | tf_op jit(solution)/shard_map/all_gather | solution.py:231
  55.7 140.7 %copy-start.26 = (f32[512,16]{0,1:T(8,128)}, f32[512,16]{0,1:T(8,128)S(1)}, u32[]{:S(2)}) copy-start(f32[512,16]{0,1:T(8,128)S(1)} %get-tuple-element.123) | copy-start | bytes 98308
  55.8 140.7 %copy-start.27 = (f32[512,16]{0,1:T(8,128)}, f32[512,16]{0,1:T(8,128)S(1)}, u32[]{:S(2)}) copy-start(f32[512,16]{0,1:T(8,128)S(1)} %get-tuple-element.122) | copy-start | bytes 98308
  122.5 72.5 %copy-start.40 = (f32[384]{0:T(512)S(1)}, f32[384]{0:T(512)}, u32[]{:S(2)}) copy-start(f32[384]{0:T(512)} %param.25) | copy-start | bytes 4612
  124.7 1.1 copy-start.11
  125.8 70.8 %copy-start.32 = (pred[512,512]{0,1:T(8,128)(4,1)S(1)}, pred[512,512]{0,1:T(8,128)(4,1)}, u32[]{:S(2)}) copy-start(pred[512,512]{0,1:T(8,128)(4,1)} %fusion.33) | copy-start | bytes 786436
  196.4 1.1 copy-start.33
  196.5 1.1 copy-start.34
  196.5 1.0 copy-start.35
  196.6 1.0 copy-start.36
  197.2 1.4 copy-start.9
  208.4 3.3 copy-start.22
  208.4 3.3 copy-start.23
  208.4 3.3 copy-start.28
  208.4 3.3 slice-start
  209.4 2.4 slice-start.1
  211.6 0.7 copy-start.16
  211.6 1.7 copy-start.10
  211.6 2.1 copy-start.12
  211.6 2.1 copy-start.41
  211.8 0.7 copy-start.4
  212.5 0.7 copy-start.6
  219.6 136.6 %all-to-all-start = ((bf16[4,512,640]{2,1,0:T(8,128)(2,1)}), bf16[4,512,640]{2,1,0:T(8,128)(2,1)S(1)}, u32[]{:S(2)}, u32[]{:S(2)}) async-start(bf16[4,512,640]{2,1,0:T(8,128)(2,1)} %stack.46), calls=%async_computation.1 | async-start | bytes 5242880 | tf_op jit(solution)/shard_map/all_to_all | solution.py:144
  229.4 149.7 %reduce-scatter.8.cloned.1.call-start = ((), (), s32[]{:S(2)}) async-start(), calls=%async_computation.9 | async-start | bytes 786432 | tf_op jit(solution)/shard_map/reduce_scatter | solution.py:238
  350.2 3.0 copy-start
  350.2 2.4 copy-start.21
  352.5 2.6 copy-start.2
  352.5 1.8 copy-start.19
  355.9 48.3 %reduce-scatter.6.cloned.1.call-start = ((), (), s32[]{:S(2)}) async-start(), calls=%async_computation.6 | async-start | bytes 393216 | tf_op jit(solution)/shard_map/reduce_scatter | solution.py:202
  356.2 2.7 copy-start.3
  361.5 1.8 copy-start.15
  361.5 1.8 copy-start.30
  364.8 3.2 copy-start.1
  364.8 90.5 %all-reduce.7.cloned.1.call-start = ((), (), s32[]{:S(2)}) async-start(), calls=%async_computation.10 | async-start | bytes 6291456 | tf_op jit(solution)/shard_map/psum | solution.py:267
  369.7 1.0 copy-start.5
  369.7 1.0 copy-start.7
  369.7 1.1 copy-start.17
  369.7 10.4 %copy-start.8 = (bf16[256,256]{1,0:T(8,128)(2,1)S(1)}, bf16[256,256]{1,0:T(8,128)(2,1)}, u32[]{:S(2)}) copy-start(bf16[256,256]{1,0:T(8,128)(2,1)} %param.16) | copy-start | bytes 393220
  369.7 10.4 %copy-start.38 = (f32[256]{0:T(256)S(1)}, f32[256]{0:T(256)}, u32[]{:S(2)}) copy-start(f32[256]{0:T(256)} %param.20) | copy-start | bytes 3076
  369.7 10.4 %copy-start.39 = (f32[256]{0:T(256)S(1)}, f32[256]{0:T(256)}, u32[]{:S(2)}) copy-start(f32[256]{0:T(256)} %param.22) | copy-start | bytes 3076
  369.8 34.4 %copy-start.25 = (bf16[256,256]{1,0:T(8,128)(2,1)S(1)}, bf16[256,256]{1,0:T(8,128)(2,1)}, u32[]{:S(2)}) copy-start(bf16[256,256]{1,0:T(8,128)(2,1)} %param.17) | copy-start | bytes 393220
  369.8 34.4 %copy-start.43 = (f32[256]{0:T(256)S(1)}, f32[256]{0:T(256)}, u32[]{:S(2)}) copy-start(f32[256]{0:T(256)} %param.31) | copy-start | bytes 3076
  369.8 34.4 %copy-start.44 = (f32[256]{0:T(256)S(1)}, f32[256]{0:T(256)}, u32[]{:S(2)}) copy-start(f32[256]{0:T(256)} %param.27) | copy-start | bytes 3076
  379.1 82.8 %copy-start.45 = (f32[256]{0:T(256)}, f32[256]{0:T(256)S(1)}, u32[]{:S(2)}) copy-start(f32[256]{0:T(256)S(1)} %convert_element_type.138) | copy-start | bytes 3076
  455.4 2.9 copy-start.13
  458.2 1.5 copy-start.24
  458.2 2.8 copy-start.31
Sparse Core Ops, SparseCore 0:
  16.5 30.1 all-gather.2
  49.4 145.5 reduce-scatter.3
  215.6 132.7 all-gather.4
  356.1 13.7 reduce-scatter.7
  371.9 11.7 reduce-scatter.5
  386.7 68.5 all-reduce.6
